TPU v7x, 128 devices: a whole 4x4x4 slice. The times are simulated.
128 devices in a mesh: row: 8 (over x, core), col: 16 (over y, z).
Axes of the slice: x: 4, y: 4, z: 4, core: 2. Of those that a mesh axis runs over, the one named last changes fastest.
Arguments:
- valence: bfloat16 [2, 16, 32768], replicated, may hold values from -6 to 6
- conduction: bfloat16 [2, 128, 32768], replicated, may hold values from -6 to 6
- valence_energy: float32 [16], replicated, may hold values from -8 to -1
- conduction_energy: float32 [128], replicated, may hold values from 0.5 to 6
- band_pairs: int32 [1024, 2], P(('row', 'col')), may hold values from 0 to 127, as said below
- grid_index: int32 [16384], replicated, may hold values from 0 to 32767, as said below
Outputs:
- response: float32 [2, 16384, 16384], P(None, 'row', 'col')
Inputs may be any that keep to these rules, and one draw needn't show every extreme that they name: `band_pairs`: the rows are distinct combinations of a valence band below 16 and a conduction band below 128, half of all combinations. `grid_index`: the 16384 entries are distinct.
All inputs are finite; a program needn't handle non-finite values.
Results may differ from a plain program's by a relative error of at most 0.0039.
Values may be sent and summed in bfloat16 or wider, within the bound.
A program may use at most 192 MiB of HBM per device.

v0:
```python
import math
import jax
import jax.numpy as jnp
from jax import lax
from jax.sharding import PartitionSpec as P

N1 = 32
N2 = 32
N3 = 32
NVB = 16
NCB = 128


def tables(length):
    position = jnp.arange(length, dtype=jnp.int32)
    phase_angle = (position[:, None] * position[None, :] % length).astype(jnp.float32) * (
        2.0 * math.pi / length
    )
    return (jnp.cos(phase_angle), jnp.sin(phase_angle))


def plane_table():
    plane_size = N2 * N3
    position = jnp.arange(plane_size, dtype=jnp.int32)
    second = position // N3
    third = position % N3
    phase_index = (
        second[:, None] * second[None, :] % N2 * N3 + third[:, None] * third[None, :] % N3 * N2
    )
    phase_angle = (phase_index % plane_size).astype(jnp.float32) * (2.0 * math.pi / plane_size)
    cosine = jnp.cos(phase_angle)
    sine_table = jnp.sin(phase_angle)
    upper = jnp.concatenate([cosine, -sine_table], axis=1)
    lower = jnp.concatenate([sine_table, cosine], axis=1)
    return jnp.concatenate([upper, lower], axis=0)


def transform(rho_real, rho_imag):
    pair_count = rho_real.shape[0]
    plane_size = N2 * N3
    stacked = jnp.concatenate(
        [
            rho_real.reshape(pair_count, N1, plane_size),
            rho_imag.reshape(pair_count, N1, plane_size),
        ],
        axis=2,
    )
    plane = jnp.dot(
        stacked.reshape(pair_count * N1, 2 * plane_size),
        plane_table(),
        precision=lax.Precision.HIGHEST,
    )
    plane = plane.reshape(pair_count, N1, 2 * plane_size)
    cosine, sine_table = tables(N1)
    cos_part = jnp.einsum("kr,prx->pkx", cosine, plane, precision=lax.Precision.HIGHEST)
    sin_part = jnp.einsum("kr,prx->pkx", sine_table, plane, precision=lax.Precision.HIGHEST)
    out_real = cos_part[:, :, :plane_size] + sin_part[:, :, plane_size:]
    out_imag = cos_part[:, :, plane_size:] - sin_part[:, :, :plane_size]
    return (out_real.reshape(pair_count, -1), out_imag.reshape(pair_count, -1))


def pair_spectrum(valence, conduction, valence_energy, conduction_energy, band_pairs):
    valence_rows = jnp.take(valence, band_pairs[:, 0], axis=1).astype(jnp.float32)
    conduction_rows = jnp.take(conduction, band_pairs[:, 1], axis=1).astype(jnp.float32)
    rho_real = valence_rows[0] * conduction_rows[0] + valence_rows[1] * conduction_rows[1]
    rho_imag = valence_rows[0] * conduction_rows[1] - valence_rows[1] * conduction_rows[0]
    out_real, out_imag = transform(rho_real, rho_imag)
    normalize = 1.0 / math.sqrt(N1 * N2 * N3)
    spectrum = jnp.stack([out_real, out_imag]) * normalize
    valence_hot = (
        band_pairs[:, 0][:, None] == jnp.arange(valence_energy.shape[0], dtype=jnp.int32)[None, :]
    )
    conduction_hot = (
        band_pairs[:, 1][:, None]
        == jnp.arange(conduction_energy.shape[0], dtype=jnp.int32)[None, :]
    )
    energy_gap = jnp.sum(jnp.where(valence_hot, valence_energy[None, :], 0.0), axis=1) - jnp.sum(
        jnp.where(conduction_hot, conduction_energy[None, :], 0.0), axis=1
    )
    weights = 2.0 / (math.sqrt(NVB * NCB // 2) * energy_gap)
    return (spectrum, weights)


def contract(weighted_part, operand, left_dims, right_dims):
    full_left = (0,) + tuple((d + 1 for d in left_dims))
    full_right = (0,) + tuple((d + 1 for d in right_dims))
    real_part = lax.dot_general(
        weighted_part,
        operand,
        ((full_left, full_right), ((), ())),
        preferred_element_type=jnp.float32,
    )
    pair_dims = ((left_dims, right_dims), ((), ()))
    imag_part = lax.dot_general(
        weighted_part[0], operand[1], pair_dims, preferred_element_type=jnp.float32
    ) - lax.dot_general(weighted_part[1], operand[0], pair_dims, preferred_element_type=jnp.float32)
    return jnp.stack([real_part, imag_part])


def body(valence, conduction, valence_energy, conduction_energy, band_pairs, grid_index):
    spectrum, weights = pair_spectrum(
        valence, conduction, valence_energy, conduction_energy, band_pairs
    )
    row_count = lax.axis_size("row")
    column_count = lax.axis_size("col")
    selected = jnp.take(spectrum, grid_index, axis=2)
    weighted = (weights[None, :, None] * selected).astype(jnp.bfloat16)
    density = selected.astype(jnp.bfloat16)
    weighted_block = lax.all_to_all(weighted, "row", split_axis=2, concat_axis=1, tiled=True)
    density_block = lax.all_to_all(density, "col", split_axis=2, concat_axis=1, tiled=True)
    weighted_all = lax.all_gather(weighted_block, "col", axis=1, tiled=True)
    density_all = lax.all_gather(density_block, "row", axis=1, tiled=True)
    pair_count = density_all.shape[1]
    per_device = pair_count // (row_count * column_count)
    weighted_split = weighted_all.reshape(
        2, column_count, row_count, per_device, weighted_all.shape[2]
    )
    density_split = density_all.reshape(
        2, row_count, column_count, per_device, density_all.shape[2]
    )
    return contract(weighted_split, density_split, (0, 1, 2), (1, 0, 2))


def solution(mesh):
    return jax.shard_map(
        body,
        mesh=mesh,
        in_specs=(P(), P(), P(), P(), P(("row", "col"), None), P()),
        out_specs=P(None, "row", "col"),
        check_vma=False,
    )
```

profile of v0, /device:TPU:1, one launch (start us, length us, event | category | flops | bytes accessed | tf_op | source)
XLA Modules:
  0.0 724.0 jit_solution(14251131210681987142)
XLA Ops:
  6.5 0.8 fusion.55
  8.2 3.6 gather_fusion.1
  11.8 1.5 convert_bitcast_fusion.1
  13.3 3.5 gather_fusion
  17.1 1.4 copy-done.2
  20.0 23.7 %fusion.25 = (f32[1024,1024]{1,0:T(8,128)}, f32[1024,1024]{1,0:T(8,128)}, f32[1024,1024]{1,0:T(8,128)}) fusion(s32[1024]{0:T(1024)S(1)} %get-tuple-element.24, s32[1024]{0:T(1024)S(1)} %get-tuple-element.25), kind=kLoop, calls=%fused_computation.53 | loop fusion | flops 41943040 | bytes 12591104 | tf_op jit(solution)/shard_map/neg | solution.py:33
  43.7 22.3 %fusion = f32[8,32,2048]{2,1,0:T(8,128)} fusion(f32[1024,1024]{1,0:T(8,128)} %get-tuple-element.15, f32[1024,1024]{1,0:T(8,128)} %get-tuple-element.14, f32[1024,1024]{1,0:T(8,128)} %get-tuple-element.13, f32[8,32,1024]{2,1,0:T(8,128)S(1)} %bitcast.102, f32[8,32,1024]{2,1,0:T(8,128)S(1)} %bitcast.103), kind=kOutput, calls=%fused_computation.4 | convolution fusion | flops 12898009088 | bytes 16777216 | tf_op jit(solution)/shard_map/dot_general | solution.py:48
  66.0 3.8 convolution_bitcast_fusion.1
  69.9 2.1 convolution_bitcast_fusion.2
  72.0 1.4 slice_add_fusion
  73.4 2.4 stack_reshape.6
  75.8 1.2 stack_reshape.7
  77.0 1.7 maximum_multiply_fusion
  78.7 28.8 %copy.31 = f32[2,8,32768]{1,0,2:T(2,128)} copy(f32[2,8,32768]{2,1,0:T(8,128)S(1)} %maximum_multiply_fusion) | data formatting | bytes 4194304 | tf_op jit(solution)/shard_map/mul | solution.py:69
  107.5 251.9 %gather_fusion.2 = f32[16384,2,8]{2,1,0:T(2,128)} fusion(f32[2,8,32768]{1,0,2:T(2,128)} %copy.31, s32[16384]{0:T(1024)S(1)} %fusion.26), kind=kCustom, calls=%fused_computation.2 | custom fusion | bytes 2162688 | tf_op jit(solution)/shard_map/jit(_take)/gather | solution.py:106
  359.4 71.1 %fusion.59 = bf16[16384,2,8]{2,1,0:T(2,128)(2,1)} fusion(f32[16384,2,8]{2,1,0:T(2,128)} %gather_fusion.2, pred[16384]{0:T(1024)(128)(4,1)S(1)} %compare_and_fusion), kind=kLoop, calls=%fused_computation.113 | loop fusion | flops 262144 | bytes 1589248
  430.5 10.5 %reshape.154 = bf16[16,2,8192]{2,1,0:T(2,128)(2,1)S(1)} reshape(bf16[16384,2,8]{2,1,0:T(2,128)(2,1)} %fusion.59) | data formatting | bytes 1048576
  440.9 18.7 %all_to_all.36 = bf16[16,2,8192]{2,1,0:T(2,128)(2,1)S(1)} all-to-all(bf16[16,2,8192]{2,1,0:T(2,128)(2,1)S(1)} %reshape.154), channel_id=1, replica_groups=mesh['row'=8,'col'=16] {'col'}, dimensions={0} | all-to-all | bytes 1048576 | tf_op jit(solution)/shard_map/all_to_all | solution.py:110
  459.6 10.9 %reshape.155 = bf16[16384,2,8]{2,1,0:T(2,128)(2,1)} reshape(bf16[16,2,8192]{2,1,0:T(2,128)(2,1)S(1)} %all_to_all.36) | data formatting | bytes 1048576
  470.6 19.3 %copy.33 = bf16[2,16,8,1024]{3,2,1,0:T(8,128)(2,1)} copy(bf16[2,16,8,1024]{2,0,3,1:T(2,128)(2,1)} %bitcast.90) | data formatting | bytes 1048576 | tf_op jit(solution)/shard_map/all_to_all | solution.py:110
  490.3 59.2 %fusion.60 = bf16[16384,2,8]{2,1,0:T(2,128)(2,1)} fusion(f32[16384,2,8]{2,1,0:T(2,128)} %gather_fusion.2, pred[16384]{0:T(1024)(128)(4,1)S(1)} %compare_and_fusion, f32[8]{0:T(128)S(1)} %multiply_divide_fusion), kind=kLoop, calls=%fused_computation.114 | loop fusion | flops 786432 | bytes 1589280
  549.4 10.4 %reshape.152 = bf16[8,2,16384]{2,1,0:T(2,128)(2,1)S(1)} reshape(bf16[16384,2,8]{2,1,0:T(2,128)(2,1)} %fusion.60) | data formatting | bytes 1048576
  559.9 15.6 %all_to_all.37 = bf16[8,2,16384]{2,1,0:T(2,128)(2,1)S(1)} all-to-all(bf16[8,2,16384]{2,1,0:T(2,128)(2,1)S(1)} %reshape.152), channel_id=1, replica_groups=mesh['row'=8,'col'=16] {'row'}, dimensions={0} | all-to-all | bytes 1048576 | tf_op jit(solution)/shard_map/all_to_all | solution.py:109
  575.5 10.9 %reshape.153 = bf16[16384,2,8]{2,1,0:T(2,128)(2,1)} reshape(bf16[8,2,16384]{2,1,0:T(2,128)(2,1)S(1)} %all_to_all.37) | data formatting | bytes 1048576
  586.3 19.2 %copy.32 = bf16[2,8,8,2048]{3,2,1,0:T(8,128)(2,1)} copy(bf16[2,8,8,2048]{2,0,3,1:T(2,128)(2,1)} %bitcast.91) | data formatting | bytes 1048576 | tf_op jit(solution)/shard_map/all_to_all | solution.py:109
  605.6 4.7 fusion.58
  610.2 62.7 %all-gather.3.cloned.1.call-done = bf16[2,1024,2048]{2,1,0:T(8,128)(2,1)} async-done(((bf16[2,64,2048]{2,1,0:T(8,128)(2,1)}), bf16[2,1024,2048]{2,1,0:T(8,128)(2,1)}) %all-gather.3.cloned.1.call-update) | async-done | bytes 8388624 | tf_op jit(solution)/shard_map/all_gather | solution.py:111
  672.9 14.5 %convolution_bitcast_fusion = f32[1,2048,1024]{2,1,0:T(8,128)} fusion(bf16[2,16,8,8,2048]{4,3,2,1,0:T(8,128)(2,1)} %bitcast.92, bf16[2,8,16,8,1024]{4,3,2,1,0:T(8,128)(2,1)} %bitcast.93), kind=kOutput, calls=%fused_computation.31 | convolution fusion | flops 8589934592 | bytes 20971520 | tf_op jit(solution)/shard_map/dot_general | solution.py:87
  687.4 5.4 fusion.57
  692.8 6.9 fusion.21
  699.8 7.4 %fusion.8 = f32[1,2048,1024]{2,1,0:T(8,128)S(1)} fusion(f32[2048,1024,1,1]{1,0,3,2:T(8,128)} %fusion.21, bf16[16,8,8,2048]{3,2,1,0:T(8,128)(2,1)S(1)} %bitcast.96, bf16[8,16,8,1024]{3,2,1,0:T(8,128)(2,1)S(1)} %bitcast.100), kind=kOutput, calls=%fused_computation.16 | convolution fusion | flops 4297064448 | bytes 23068672 | tf_op jit(solution)/shard_map/dot_general | solution.py:96
  707.2 10.0 %pad_maximum_fusion = f32[2,2048,1024]{2,1,0:T(8,128)} fusion(f32[1,2048,1024]{2,1,0:T(8,128)S(1)} %fusion.8, f32[1,2048,1024]{2,1,0:T(8,128)} %convolution_bitcast_fusion), kind=kLoop, calls=%fused_computation.11 | loop fusion | flops 4194304 | bytes 33554432 | tf_op jit(solution)/shard_map/stack | solution.py:97
  (36 shorter events, 3.1 us)
Async XLA Ops:
  6.5 6.8 copy-start
  6.5 599.0 %all-gather.5.cloned.1.call-start = ((), (), s32[]{:S(2)}) async-start(), calls=%async_computation.3 | async-start | bytes 4718592 | tf_op jit(solution)/shard_map/all_gather | solution.py:112
  16.9 1.6 copy-start.2
  66.0 3.8 copy-start.3
  66.0 6.0 copy-start.7
  470.6 19.3 %copy-start.8 = (f32[128]{0:T(128)S(1)}, f32[128]{0:T(128)}, u32[]{:S(2)}) copy-start(f32[128]{0:T(128)} %param.9) | copy-start | bytes 1540
  470.6 19.5 %copy-start.9 = (f32[16]{0:T(128)S(1)}, f32[16]{0:T(128)}, u32[]{:S(2)}) copy-start(f32[16]{0:T(128)} %param.8) | copy-start | bytes 196
  489.8 183.1 %all-gather.3.cloned.1.call-start = ((), (), s32[]{:S(2)}) async-start(), calls=%async_computation.2 | async-start | bytes 8912896 | tf_op jit(solution)/shard_map/all_gather | solution.py:111
  687.4 5.4 copy-start.6
  692.8 7.0 copy-start.4
  692.8 7.0 copy-start.5
  707.1 10.0 %copy-start.1 = (bf16[2,16,32768]{2,1,0:T(8,128)(2,1)S(1)}, bf16[2,16,32768]{2,1,0:T(8,128)(2,1)}, u32[]{:S(2)}) copy-start(bf16[2,16,32768]{2,1,0:T(8,128)(2,1)} %param.6) | copy-start | bytes 6291460
Sparse Core Ops, SparseCore 0:
  490.0 31.7 all-gather.4
  605.7 67.1 all-gather.2
where the time goes:
time: 734 us; the launch traced here: 724 us
  local copies, waits for them, and re-layouts  385 us (52%)
  other arithmetic  171 us (23%)
  waiting for transfers between devices  62.7 us (9%)
  matrix products  57 us (8%)
  blocking collectives  34.3 us (5%)
  between operations  13.6 us (2%)
    gather x1, local copies, waits for them, and re-layouts, body(): selected = jnp.take(spectrum, grid_index, axis=2)  252 us
    unnamed x2, other arithmetic  130 us
    all_gather x1, waiting for transfers between devices, body(): weighted_all = lax.all_gather(weighted_block, 'col', axis=1, tiled=True)  62.7 us
    unnamed x26, local copies, waits for them, and re-layouts  45.3 us
    mul x1, local copies, waits for them, and re-layouts, pair_spectrum(): spectrum = jnp.stack([out_real, out_imag]) * normalize  28.8 us
    neg x1, other arithmetic, plane_table(): upper = jnp.concatenate([cosine, -sine_table], axis=1)  23.7 us
    dot_general x1, matrix products, transform(): jnp.dot(stacked.reshape(pair_count * N1, 2 * plane_size), plane_table(),...  22.3 us
    all_to_all x1, local copies, waits for them, and re-layouts, body(): lax.all_to_all(density, 'col', split_axis=2, concat_axis=1, tiled=True)  19.3 us
  transfers between devices with their start and end apart: 2, of which 1 were waited for; matrix products, arithmetic and copies ran while one was open for 14% of the time, Pallas kernels for 0%

commit v1 on v0

--- a/solution.py
+++ b/solution.py
@@ -108,7 +108,15 @@
     density = selected.astype(jnp.bfloat16)
     weighted_block = lax.all_to_all(weighted, "row", split_axis=2, concat_axis=1, tiled=True)
     density_block = lax.all_to_all(density, "col", split_axis=2, concat_axis=1, tiled=True)
-    weighted_all = lax.all_gather(weighted_block, "col", axis=1, tiled=True)
+    pool = [weighted_block]
+    n_parts = lax.psum(1, "col")
+    for src_i in range(n_parts - 1):
+        pool.append(
+            lax.ppermute(pool[-1], "col", [(to_i, (to_i + 1) % n_parts) for to_i in range(n_parts)])
+        )
+    weighted_all = jnp.roll(
+        jnp.concatenate(pool[::-1], 1), (lax.axis_index("col") + 1) * weighted_block.shape[1], 1
+    )
     density_all = lax.all_gather(density_block, "row", axis=1, tiled=True)
     pair_count = density_all.shape[1]
     per_device = pair_count // (row_count * column_count)

time: 734 us -> 896 us (1.22)
  the two profiles are of different devices: /device:TPU:1 before, /device:TPU:0 now
where the time goes in v1:
time: 896 us; the launch traced here: 886 us
  local copies, waits for them, and re-layouts  433 us (48%)
  waiting for transfers between devices  204 us (23%)
  other arithmetic  159 us (18%)
  matrix products  60.4 us (7%)
  starting transfers between devices  16 us (2%)
  between operations  13.9 us (2%)
    gather x1, local copies, waits for them, and re-layouts, body(): selected = jnp.take(spectrum, grid_index, axis=2)  252 us
    ppermute x15, waiting for transfers between devices, body(): lax.ppermute(pool[-1], 'col', [(to_i, (to_i + 1) % n_parts) for to_i in r...  204 us
    unnamed x2, other arithmetic  118 us
    unnamed x87, local copies, waits for them, and re-layouts  82 us
    mul x1, local copies, waits for them, and re-layouts, pair_spectrum(): spectrum = jnp.stack([out_real, out_imag]) * normalize  28.8 us
    neg x1, other arithmetic, plane_table(): upper = jnp.concatenate([cosine, -sine_table], axis=1)  23.9 us
    dot_general x1, matrix products, transform(): jnp.dot(stacked.reshape(pair_count * N1, 2 * plane_size), plane_table(),...  22.3 us
    all_to_all x1, local copies, waits for them, and re-layouts, body(): lax.all_to_all(density, 'col', split_axis=2, concat_axis=1, tiled=True)  19.2 us
  transfers between devices with their start and end apart: 18, of which 14 were waited for; matrix products, arithmetic and copies ran while one was open for 15% of the time, Pallas kernels for 0%

profile of v1, /device:TPU:0, one launch (start us, length us, event | category | flops | bytes accessed | tf_op | source)
XLA Modules:
  0.0 885.6 jit_solution(4470813232845200093)
XLA Ops:
  21.8 23.9 %fusion.25 = (f32[1024,1024]{1,0:T(8,128)}, f32[1024,1024]{1,0:T(8,128)}, f32[1024,1024]{1,0:T(8,128)}) fusion(s32[1024]{0:T(1024)S(1)} %get-tuple-element.22, s32[1024]{0:T(1024)S(1)} %get-tuple-element.23), kind=kLoop, calls=%fused_computation.53 | loop fusion | flops 41943040 | bytes 12591104 | tf_op jit(solution)/shard_map/neg | solution.py:33
  45.7 22.3 %fusion = f32[8,32,2048]{2,1,0:T(8,128)} fusion(f32[1024,1024]{1,0:T(8,128)} %get-tuple-element.15, f32[1024,1024]{1,0:T(8,128)} %get-tuple-element.14, f32[1024,1024]{1,0:T(8,128)} %get-tuple-element.13, f32[8,32,1024]{2,1,0:T(8,128)S(1)} %bitcast.105, f32[8,32,1024]{2,1,0:T(8,128)S(1)} %bitcast.104), kind=kOutput, calls=%fused_computation.4 | convolution fusion | flops 12898009088 | bytes 16777216 | tf_op jit(solution)/shard_map/dot_general | solution.py:48
  82.0 28.8 %copy.31 = f32[2,8,32768]{1,0,2:T(2,128)} copy(f32[2,8,32768]{2,1,0:T(8,128)S(1)} %maximum_multiply_fusion) | data formatting | bytes 4194304 | tf_op jit(solution)/shard_map/mul | solution.py:69
  111.2 251.9 %gather_fusion.2 = f32[16384,2,8]{2,1,0:T(2,128)} fusion(f32[2,8,32768]{1,0,2:T(2,128)} %copy.31, s32[16384]{0:T(1024)S(1)} %fusion.26), kind=kCustom, calls=%fused_computation.2 | custom fusion | bytes 2162688 | tf_op jit(solution)/shard_map/jit(_take)/gather | solution.py:106
  363.0 59.3 %fusion.59 = bf16[16384,2,8]{2,1,0:T(2,128)(2,1)} fusion(f32[16384,2,8]{2,1,0:T(2,128)} %gather_fusion.2, pred[16384]{0:T(1024)(128)(4,1)S(1)} %compare_and_fusion, f32[8]{0:T(128)S(1)} %multiply_divide_fusion), kind=kLoop, calls=%fused_computation.148 | loop fusion | flops 786432 | bytes 1589280
  422.3 11.2 %reshape.152 = bf16[8,2,16384]{2,1,0:T(2,128)(2,1)} reshape(bf16[16384,2,8]{2,1,0:T(2,128)(2,1)} %fusion.59) | data formatting | bytes 1048576
  437.9 59.1 %fusion.58 = bf16[16384,2,8]{2,1,0:T(2,128)(2,1)} fusion(f32[16384,2,8]{2,1,0:T(2,128)} %gather_fusion.2, pred[16384]{0:T(1024)(128)(4,1)S(1)} %compare_and_fusion), kind=kLoop, calls=%fused_computation.147 | loop fusion | flops 262144 | bytes 1589248
  497.0 11.2 %reshape.154 = bf16[16,2,8192]{2,1,0:T(2,128)(2,1)} reshape(bf16[16384,2,8]{2,1,0:T(2,128)(2,1)} %fusion.58) | data formatting | bytes 1048576
  508.2 8.0 all-to-all-start.1
  516.3 10.9 %reshape.153 = bf16[16384,2,8]{2,1,0:T(2,128)(2,1)} reshape(bf16[8,2,16384]{2,1,0:T(2,128)(2,1)S(1)} %all-to-all-done) | data formatting | bytes 1048576
  527.2 17.7 %copy.32 = bf16[2,8,8,2048]{3,2,1,0:T(8,128)(2,1)S(1)} copy(bf16[2,8,8,2048]{2,0,3,1:T(2,128)(2,1)} %bitcast.92) | data formatting | bytes 1048576 | tf_op jit(solution)/shard_map/all_to_all | solution.py:109
  546.8 10.9 %reshape.155 = bf16[16384,2,8]{2,1,0:T(2,128)(2,1)} reshape(bf16[16,2,8192]{2,1,0:T(2,128)(2,1)S(1)} %all-to-all-done.1) | data formatting | bytes 1048576
  557.7 19.2 %copy.33 = bf16[2,16,8,1024]{3,2,1,0:T(8,128)(2,1)} copy(bf16[2,16,8,1024]{2,0,3,1:T(2,128)(2,1)} %bitcast.93) | data formatting | bytes 1048576 | tf_op jit(solution)/shard_map/all_to_all | solution.py:110
  578.5 15.4 %collective-permute-done.1 = bf16[2,64,2048]{2,1,0:T(8,128)(2,1)S(1)} collective-permute-done((bf16[2,64,2048]{2,1,0:T(8,128)(2,1)S(1)}, bf16[2,64,2048]{2,1,0:T(8,128)(2,1)S(1)}, u32[]{:S(2)}, u32[]{:S(2)}) %collective-permute-start.1) | collective-permute-done | bytes 524320 | tf_op jit(solution)/shard_map/ppermute | solution.py:115
  593.8 15.9 %collective-permute-done.2 = bf16[2,64,2048]{2,1,0:T(8,128)(2,1)S(1)} collective-permute-done((bf16[2,64,2048]{2,1,0:T(8,128)(2,1)S(1)}, bf16[2,64,2048]{2,1,0:T(8,128)(2,1)S(1)}, u32[]{:S(2)}, u32[]{:S(2)}) %collective-permute-start.2) | collective-permute-done | bytes 524320 | tf_op jit(solution)/shard_map/ppermute | solution.py:115
  609.7 15.0 %collective-permute-done.3 = bf16[2,64,2048]{2,1,0:T(8,128)(2,1)S(1)} collective-permute-done((bf16[2,64,2048]{2,1,0:T(8,128)(2,1)S(1)}, bf16[2,64,2048]{2,1,0:T(8,128)(2,1)S(1)}, u32[]{:S(2)}, u32[]{:S(2)}) %collective-permute-start.3) | collective-permute-done | bytes 524320 | tf_op jit(solution)/shard_map/ppermute | solution.py:115
  624.7 14.1 %collective-permute-done.4 = bf16[2,64,2048]{2,1,0:T(8,128)(2,1)S(1)} collective-permute-done((bf16[2,64,2048]{2,1,0:T(8,128)(2,1)S(1)}, bf16[2,64,2048]{2,1,0:T(8,128)(2,1)S(1)}, u32[]{:S(2)}, u32[]{:S(2)}) %collective-permute-start.4) | collective-permute-done | bytes 524320 | tf_op jit(solution)/shard_map/ppermute | solution.py:115
  638.8 13.2 %collective-permute-done.5 = bf16[2,64,2048]{2,1,0:T(8,128)(2,1)S(1)} collective-permute-done((bf16[2,64,2048]{2,1,0:T(8,128)(2,1)S(1)}, bf16[2,64,2048]{2,1,0:T(8,128)(2,1)S(1)}, u32[]{:S(2)}, u32[]{:S(2)}) %collective-permute-start.5) | collective-permute-done | bytes 524320 | tf_op jit(solution)/shard_map/ppermute | solution.py:115
  652.8 12.5 %collective-permute-done.6 = bf16[2,64,2048]{2,1,0:T(8,128)(2,1)S(1)} collective-permute-done((bf16[2,64,2048]{2,1,0:T(8,128)(2,1)S(1)}, bf16[2,64,2048]{2,1,0:T(8,128)(2,1)S(1)}, u32[]{:S(2)}, u32[]{:S(2)}) %collective-permute-start.6) | collective-permute-done | bytes 524320 | tf_op jit(solution)/shard_map/ppermute | solution.py:115
  666.1 12.9 %collective-permute-done.7 = bf16[2,64,2048]{2,1,0:T(8,128)(2,1)S(1)} collective-permute-done((bf16[2,64,2048]{2,1,0:T(8,128)(2,1)S(1)}, bf16[2,64,2048]{2,1,0:T(8,128)(2,1)S(1)}, u32[]{:S(2)}, u32[]{:S(2)}) %collective-permute-start.7) | collective-permute-done | bytes 524320 | tf_op jit(solution)/shard_map/ppermute | solution.py:115
  679.8 14.0 %collective-permute-done.8 = bf16[2,64,2048]{2,1,0:T(8,128)(2,1)S(1)} collective-permute-done((bf16[2,64,2048]{2,1,0:T(8,128)(2,1)S(1)}, bf16[2,64,2048]{2,1,0:T(8,128)(2,1)S(1)}, u32[]{:S(2)}, u32[]{:S(2)}) %collective-permute-start.8) | collective-permute-done | bytes 524320 | tf_op jit(solution)/shard_map/ppermute | solution.py:115
  694.7 15.1 %collective-permute-done.9 = bf16[2,64,2048]{2,1,0:T(8,128)(2,1)S(1)} collective-permute-done((bf16[2,64,2048]{2,1,0:T(8,128)(2,1)S(1)}, bf16[2,64,2048]{2,1,0:T(8,128)(2,1)S(1)}, u32[]{:S(2)}, u32[]{:S(2)}) %collective-permute-start.9) | collective-permute-done | bytes 524320 | tf_op jit(solution)/shard_map/ppermute | solution.py:115
  710.5 16.2 %collective-permute-done.10 = bf16[2,64,2048]{2,1,0:T(8,128)(2,1)S(1)} collective-permute-done((bf16[2,64,2048]{2,1,0:T(8,128)(2,1)S(1)}, bf16[2,64,2048]{2,1,0:T(8,128)(2,1)S(1)}, u32[]{:S(2)}, u32[]{:S(2)}) %collective-permute-start.10) | collective-permute-done | bytes 524320 | tf_op jit(solution)/shard_map/ppermute | solution.py:115
  727.5 17.3 %collective-permute-done.11 = bf16[2,64,2048]{2,1,0:T(8,128)(2,1)S(1)} collective-permute-done((bf16[2,64,2048]{2,1,0:T(8,128)(2,1)S(1)}, bf16[2,64,2048]{2,1,0:T(8,128)(2,1)S(1)}, u32[]{:S(2)}, u32[]{:S(2)}) %collective-permute-start.11) | collective-permute-done | bytes 524320 | tf_op jit(solution)/shard_map/ppermute | solution.py:115
  745.7 17.7 %collective-permute-done.12 = bf16[2,64,2048]{2,1,0:T(8,128)(2,1)S(1)} collective-permute-done((bf16[2,64,2048]{2,1,0:T(8,128)(2,1)S(1)}, bf16[2,64,2048]{2,1,0:T(8,128)(2,1)S(1)}, u32[]{:S(2)}, u32[]{:S(2)}) %collective-permute-start.12) | collective-permute-done | bytes 524320 | tf_op jit(solution)/shard_map/ppermute | solution.py:115
  764.2 16.5 %collective-permute-done.13 = bf16[2,64,2048]{2,1,0:T(8,128)(2,1)} collective-permute-done((bf16[2,64,2048]{2,1,0:T(8,128)(2,1)S(1)}, bf16[2,64,2048]{2,1,0:T(8,128)(2,1)}, u32[]{:S(2)}, u32[]{:S(2)}) %collective-permute-start.13) | collective-permute-done | bytes 524320 | tf_op jit(solution)/shard_map/ppermute | solution.py:115
  785.6 7.9 collective-permute-done.14
  824.6 8.3 constant_dynamic-slice_fusion.2
  832.9 8.5 constant_dynamic-slice_fusion
  841.4 13.2 %convolution_bitcast_fusion = f32[1,2048,1024]{2,1,0:T(8,128)} fusion(bf16[2,16,8,8,2048]{4,3,2,1,0:T(8,128)(2,1)S(1)} %bitcast.94, bf16[2,8,16,8,1024]{4,3,2,1,0:T(8,128)(2,1)} %bitcast.96), kind=kOutput, calls=%fused_computation.31 | convolution fusion | flops 8589934592 | bytes 20971520 | tf_op jit(solution)/shard_map/dot_general | solution.py:87
  854.6 6.9 fusion.21
  861.5 10.8 %fusion.8 = f32[1,2048,1024]{2,1,0:T(8,128)S(1)} fusion(f32[2048,1024,1,1]{1,0,3,2:T(8,128)} %fusion.21, bf16[16,8,8,2048]{3,2,1,0:T(8,128)(2,1)} %bitcast.99, bf16[8,16,8,1024]{3,2,1,0:T(8,128)(2,1)S(1)} %bitcast.102), kind=kOutput, calls=%fused_computation.16 | convolution fusion | flops 4297064448 | bytes 23068672 | tf_op jit(solution)/shard_map/dot_general | solution.py:96
  (128 shorter events, 86.2 us)
Async XLA Ops:
  6.5 8.5 copy-start
  82.0 28.8 %copy-start.23 = (f32[128]{0:T(128)S(1)}, f32[128]{0:T(128)}, u32[]{:S(2)}) copy-start(f32[128]{0:T(128)} %param.9) | copy-start | bytes 1540
  82.0 29.0 %copy-start.24 = (f32[16]{0:T(128)S(1)}, f32[16]{0:T(128)}, u32[]{:S(2)}) copy-start(f32[16]{0:T(128)} %param.8) | copy-start | bytes 196
  433.5 74.7 %all-to-all-start = ((bf16[8,2,16384]{2,1,0:T(2,128)(2,1)}), bf16[8,2,16384]{2,1,0:T(2,128)(2,1)S(1)}, u32[]{:S(2)}, u32[]{:S(2)}) async-start(bf16[8,2,16384]{2,1,0:T(2,128)(2,1)} %reshape.152), calls=%async_computation | async-start | bytes 1048576 | tf_op jit(solution)/shard_map/all_to_all | solution.py:109
  508.2 38.6 %all-to-all-start.1 = ((bf16[16,2,8192]{2,1,0:T(2,128)(2,1)}), bf16[16,2,8192]{2,1,0:T(2,128)(2,1)S(1)}, u32[]{:S(2)}, u32[]{:S(2)}) async-start(bf16[16,2,8192]{2,1,0:T(2,128)(2,1)} %reshape.154), calls=%async_computation.1 | async-start | bytes 1048576 | tf_op jit(solution)/shard_map/all_to_all | solution.py:110
  516.2 264.5 %all-gather.2.cloned.1.call-start = ((), (), s32[]{:S(2)}) async-start(), calls=%async_computation.2 | async-start | bytes 4718592 | tf_op jit(solution)/shard_map/all_gather | solution.py:120
  544.8 32.1 %collective-permute-start = (bf16[2,64,2048]{2,1,0:T(8,128)(2,1)S(1)}, bf16[2,64,2048]{2,1,0:T(8,128)(2,1)S(1)}, u32[]{:S(2)}, u32[]{:S(2)}) collective-permute-start(bf16[2,64,2048]{2,1,0:T(8,128)(2,1)S(1)} %bitcast.95), channel_id=1, source_target_pairs={{0,1},{1,2},{2,3},{3,4},{4,5},{5,6},{6,7},{7,8},{8,9},{9,10},{10,1... | collective-permute-start | bytes 1572872 | tf_op jit(solution)/shard_map/ppermute | solution.py:115
  576.9 16.9 %collective-permute-start.1 = (bf16[2,64,2048]{2,1,0:T(8,128)(2,1)S(1)}, bf16[2,64,2048]{2,1,0:T(8,128)(2,1)S(1)}, u32[]{:S(2)}, u32[]{:S(2)}) collective-permute-start(bf16[2,64,2048]{2,1,0:T(8,128)(2,1)S(1)} %collective-permute-done), channel_id=1, source_target_pairs={{0,1},{1,2},{2,3},{3,4},{4,5},{5,6},{6,7},{7,8},{8,9},{9,10},{10,1... | collective-permute-start | bytes 1572872 | tf_op jit(solution)/shard_map/ppermute | solution.py:115
  593.8 15.9 %collective-permute-start.2 = (bf16[2,64,2048]{2,1,0:T(8,128)(2,1)S(1)}, bf16[2,64,2048]{2,1,0:T(8,128)(2,1)S(1)}, u32[]{:S(2)}, u32[]{:S(2)}) collective-permute-start(bf16[2,64,2048]{2,1,0:T(8,128)(2,1)S(1)} %collective-permute-done.1), channel_id=1, source_target_pairs={{0,1},{1,2},{2,3},{3,4},{4,5},{5,6},{6,7},{7,8},{8,9},{9,10},{10,1... | collective-permute-start | bytes 1572872 | tf_op jit(solution)/shard_map/ppermute | solution.py:115
  609.7 15.0 %collective-permute-start.3 = (bf16[2,64,2048]{2,1,0:T(8,128)(2,1)S(1)}, bf16[2,64,2048]{2,1,0:T(8,128)(2,1)S(1)}, u32[]{:S(2)}, u32[]{:S(2)}) collective-permute-start(bf16[2,64,2048]{2,1,0:T(8,128)(2,1)S(1)} %collective-permute-done.2), channel_id=1, source_target_pairs={{0,1},{1,2},{2,3},{3,4},{4,5},{5,6},{6,7},{7,8},{8,9},{9,10},{10,1... | collective-permute-start | bytes 1572872 | tf_op jit(solution)/shard_map/ppermute | solution.py:115
  624.7 14.1 %collective-permute-start.4 = (bf16[2,64,2048]{2,1,0:T(8,128)(2,1)S(1)}, bf16[2,64,2048]{2,1,0:T(8,128)(2,1)S(1)}, u32[]{:S(2)}, u32[]{:S(2)}) collective-permute-start(bf16[2,64,2048]{2,1,0:T(8,128)(2,1)S(1)} %collective-permute-done.3), channel_id=1, source_target_pairs={{0,1},{1,2},{2,3},{3,4},{4,5},{5,6},{6,7},{7,8},{8,9},{9,10},{10,1... | collective-permute-start | bytes 1572872 | tf_op jit(solution)/shard_map/ppermute | solution.py:115
  638.8 13.2 %collective-permute-start.5 = (bf16[2,64,2048]{2,1,0:T(8,128)(2,1)S(1)}, bf16[2,64,2048]{2,1,0:T(8,128)(2,1)S(1)}, u32[]{:S(2)}, u32[]{:S(2)}) collective-permute-start(bf16[2,64,2048]{2,1,0:T(8,128)(2,1)S(1)} %collective-permute-done.4), channel_id=1, source_target_pairs={{0,1},{1,2},{2,3},{3,4},{4,5},{5,6},{6,7},{7,8},{8,9},{9,10},{10,1... | collective-permute-start | bytes 1572872 | tf_op jit(solution)/shard_map/ppermute | solution.py:115
  652.8 12.5 %collective-permute-start.6 = (bf16[2,64,2048]{2,1,0:T(8,128)(2,1)S(1)}, bf16[2,64,2048]{2,1,0:T(8,128)(2,1)S(1)}, u32[]{:S(2)}, u32[]{:S(2)}) collective-permute-start(bf16[2,64,2048]{2,1,0:T(8,128)(2,1)S(1)} %collective-permute-done.5), channel_id=1, source_target_pairs={{0,1},{1,2},{2,3},{3,4},{4,5},{5,6},{6,7},{7,8},{8,9},{9,10},{10,1... | collective-permute-start | bytes 1572872 | tf_op jit(solution)/shard_map/ppermute | solution.py:115
  666.1 12.9 %collective-permute-start.7 = (bf16[2,64,2048]{2,1,0:T(8,128)(2,1)S(1)}, bf16[2,64,2048]{2,1,0:T(8,128)(2,1)S(1)}, u32[]{:S(2)}, u32[]{:S(2)}) collective-permute-start(bf16[2,64,2048]{2,1,0:T(8,128)(2,1)S(1)} %collective-permute-done.6), channel_id=1, source_target_pairs={{0,1},{1,2},{2,3},{3,4},{4,5},{5,6},{6,7},{7,8},{8,9},{9,10},{10,1... | collective-permute-start | bytes 1572872 | tf_op jit(solution)/shard_map/ppermute | solution.py:115
  679.8 14.0 %collective-permute-start.8 = (bf16[2,64,2048]{2,1,0:T(8,128)(2,1)S(1)}, bf16[2,64,2048]{2,1,0:T(8,128)(2,1)S(1)}, u32[]{:S(2)}, u32[]{:S(2)}) collective-permute-start(bf16[2,64,2048]{2,1,0:T(8,128)(2,1)S(1)} %collective-permute-done.7), channel_id=1, source_target_pairs={{0,1},{1,2},{2,3},{3,4},{4,5},{5,6},{6,7},{7,8},{8,9},{9,10},{10,1... | collective-permute-start | bytes 1572872 | tf_op jit(solution)/shard_map/ppermute | solution.py:115
  694.6 15.1 %collective-permute-start.9 = (bf16[2,64,2048]{2,1,0:T(8,128)(2,1)S(1)}, bf16[2,64,2048]{2,1,0:T(8,128)(2,1)S(1)}, u32[]{:S(2)}, u32[]{:S(2)}) collective-permute-start(bf16[2,64,2048]{2,1,0:T(8,128)(2,1)S(1)} %collective-permute-done.8), channel_id=1, source_target_pairs={{0,1},{1,2},{2,3},{3,4},{4,5},{5,6},{6,7},{7,8},{8,9},{9,10},{10,1... | collective-permute-start | bytes 1572872 | tf_op jit(solution)/shard_map/ppermute | solution.py:115
  710.5 16.2 %collective-permute-start.10 = (bf16[2,64,2048]{2,1,0:T(8,128)(2,1)S(1)}, bf16[2,64,2048]{2,1,0:T(8,128)(2,1)S(1)}, u32[]{:S(2)}, u32[]{:S(2)}) collective-permute-start(bf16[2,64,2048]{2,1,0:T(8,128)(2,1)S(1)} %collective-permute-done.9), channel_id=1, source_target_pairs={{0,1},{1,2},{2,3},{3,4},{4,5},{5,6},{6,7},{7,8},{8,9},{9,10},{10,1... | collective-permute-start | bytes 1572872 | tf_op jit(solution)/shard_map/ppermute | solution.py:115
  727.5 17.3 %collective-permute-start.11 = (bf16[2,64,2048]{2,1,0:T(8,128)(2,1)S(1)}, bf16[2,64,2048]{2,1,0:T(8,128)(2,1)S(1)}, u32[]{:S(2)}, u32[]{:S(2)}) collective-permute-start(bf16[2,64,2048]{2,1,0:T(8,128)(2,1)S(1)} %collective-permute-done.10), channel_id=1, source_target_pairs={{0,1},{1,2},{2,3},{3,4},{4,5},{5,6},{6,7},{7,8},{8,9},{9,10},{10,1... | collective-permute-start | bytes 1572872 | tf_op jit(solution)/shard_map/ppermute | solution.py:115
  745.7 17.7 %collective-permute-start.12 = (bf16[2,64,2048]{2,1,0:T(8,128)(2,1)S(1)}, bf16[2,64,2048]{2,1,0:T(8,128)(2,1)S(1)}, u32[]{:S(2)}, u32[]{:S(2)}) collective-permute-start(bf16[2,64,2048]{2,1,0:T(8,128)(2,1)S(1)} %collective-permute-done.11), channel_id=1, source_target_pairs={{0,1},{1,2},{2,3},{3,4},{4,5},{5,6},{6,7},{7,8},{8,9},{9,10},{10,1... | collective-permute-start | bytes 1572872 | tf_op jit(solution)/shard_map/ppermute | solution.py:115
  764.2 16.5 %collective-permute-start.13 = (bf16[2,64,2048]{2,1,0:T(8,128)(2,1)S(1)}, bf16[2,64,2048]{2,1,0:T(8,128)(2,1)}, u32[]{:S(2)}, u32[]{:S(2)}) collective-permute-start(bf16[2,64,2048]{2,1,0:T(8,128)(2,1)S(1)} %collective-permute-done.12), channel_id=1, source_target_pairs={{0,1},{1,2},{2,3},{3,4},{4,5},{5,6},{6,7},{7,8},{8,9},{9,10},{10,1... | collective-permute-start | bytes 1572872 | tf_op jit(solution)/shard_map/ppermute | solution.py:115
  780.7 12.8 %collective-permute-start.14 = (bf16[2,64,2048]{2,1,0:T(8,128)(2,1)}, bf16[2,64,2048]{2,1,0:T(8,128)(2,1)}, u32[]{:S(2)}, u32[]{:S(2)}) collective-permute-start(bf16[2,64,2048]{2,1,0:T(8,128)(2,1)} %collective-permute-done.13), channel_id=1, source_target_pairs={{0,1},{1,2},{2,3},{3,4},{4,5},{5,6},{6,7},{7,8},{8,9},{9,10},{10,1... | collective-permute-start | bytes 1572872 | tf_op jit(solution)/shard_map/ppermute | solution.py:115
  780.7 16.6 %copy-start.20 = (bf16[2,64,2048]{2,1,0:T(8,128)(2,1)S(1)}, bf16[2,64,2048]{2,1,0:T(8,128)(2,1)}, u32[]{:S(2)}) copy-start(bf16[2,64,2048]{2,1,0:T(8,128)(2,1)} %copy-done.19) | copy-start | bytes 1572868
  780.7 17.4 %copy-start.18 = (bf16[2,64,2048]{2,1,0:T(8,128)(2,1)S(1)}, bf16[2,64,2048]{2,1,0:T(8,128)(2,1)}, u32[]{:S(2)}) copy-start(bf16[2,64,2048]{2,1,0:T(8,128)(2,1)} %copy-done.17) | copy-start | bytes 1572868
  780.7 18.3 %copy-start.16 = (bf16[2,64,2048]{2,1,0:T(8,128)(2,1)S(1)}, bf16[2,64,2048]{2,1,0:T(8,128)(2,1)}, u32[]{:S(2)}) copy-start(bf16[2,64,2048]{2,1,0:T(8,128)(2,1)} %copy-done.15) | copy-start | bytes 1572868
  780.7 19.1 %copy-start.14 = (bf16[2,64,2048]{2,1,0:T(8,128)(2,1)S(1)}, bf16[2,64,2048]{2,1,0:T(8,128)(2,1)}, u32[]{:S(2)}) copy-start(bf16[2,64,2048]{2,1,0:T(8,128)(2,1)} %copy-done.13) | copy-start | bytes 1572868
  780.8 19.9 %copy-start.12 = (bf16[2,64,2048]{2,1,0:T(8,128)(2,1)S(1)}, bf16[2,64,2048]{2,1,0:T(8,128)(2,1)}, u32[]{:S(2)}) copy-start(bf16[2,64,2048]{2,1,0:T(8,128)(2,1)} %copy-done.11) | copy-start | bytes 1572868
  780.8 20.8 %copy-start.10 = (bf16[2,64,2048]{2,1,0:T(8,128)(2,1)S(1)}, bf16[2,64,2048]{2,1,0:T(8,128)(2,1)}, u32[]{:S(2)}) copy-start(bf16[2,64,2048]{2,1,0:T(8,128)(2,1)} %copy-done.9) | copy-start | bytes 1572868
  780.8 21.6 %copy-start.8 = (bf16[2,64,2048]{2,1,0:T(8,128)(2,1)S(1)}, bf16[2,64,2048]{2,1,0:T(8,128)(2,1)}, u32[]{:S(2)}) copy-start(bf16[2,64,2048]{2,1,0:T(8,128)(2,1)} %copy-done.7) | copy-start | bytes 1572868
  780.8 22.4 %copy-start.6 = (bf16[2,64,2048]{2,1,0:T(8,128)(2,1)S(1)}, bf16[2,64,2048]{2,1,0:T(8,128)(2,1)}, u32[]{:S(2)}) copy-start(bf16[2,64,2048]{2,1,0:T(8,128)(2,1)} %copy-done.5) | copy-start | bytes 1572868
  841.4 13.2 %copy-start.4 = (bf16[1,1024,2048]{2,1,0:T(8,128)(2,1)S(1)}, bf16[1,1024,2048]{2,1,0:T(8,128)(2,1)}, u32[]{:S(2)}) copy-start(bf16[1,1024,2048]{2,1,0:T(8,128)(2,1)} %get-tuple-element.6) | copy-start | bytes 12582916
  841.4 13.2 %copy-start.22 = (bf16[1,1024,1024]{2,1,0:T(8,128)(2,1)S(1)}, bf16[1,1024,1024]{2,1,0:T(8,128)(2,1)}, u32[]{:S(2)}) copy-start(bf16[1,1024,1024]{2,1,0:T(8,128)(2,1)} %get-tuple-element.8) | copy-start | bytes 6291460
  861.5 10.8 %copy-start.3 = (f32[1,2048,1024]{2,1,0:T(8,128)S(1)}, f32[1,2048,1024]{2,1,0:T(8,128)}, u32[]{:S(2)}) copy-start(f32[1,2048,1024]{2,1,0:T(8,128)} %convolution_bitcast_fusion) | copy-start | bytes 25165828
  (11 other events, 28.1 us)
Sparse Core Ops, SparseCore 0:
  577.0 33.3 all-gather.1
